TPU v7x, 32 devices: a whole 2x2x4 slice. The times are simulated.
32 devices in a mesh: area: 16 (over z, y, core), depth: 2 (over x).
Axes of the slice: x: 2, y: 2, z: 4, core: 2. Of those that a mesh axis runs over, the one named last changes fastest.
Arguments:
- pressure: float32 [32, 128, 1024], P('depth', 'area'), may hold values from -2.5 to -0.3
- theta_old: float32 [32, 128, 1024], P('depth', 'area'), may hold values from 0.1 to 0.35
- source: float32 [32, 128, 1024], P('depth', 'area'), may hold values from -3 to 3
- soil_type: int32 [32, 128, 1024], P('depth', 'area'), may hold values from 0 to 11
- soil_params: float32 [5, 12], replicated, as said below
Outputs:
- new_pressure: float32 [32, 128, 1024], P('depth', 'area')
- coarse_head: float32 [128, 1024], P('area')
Inputs may be any that keep to these rules, and one draw needn't show every extreme that they name: Each column of soil_params holds theta_r in 0.03 to 0.1, theta_s in 0.35 to 0.5, a in 0.5 to 3, n in 1.3 to 2.5, Ks in 0.2 to 2.
All inputs are finite; a program needn't handle non-finite values.
Results may differ from a plain program's by a relative error of at most 0.00002.
Values sent between devices are 32-bit elements; how exact they have to be, the bound alone decides.
No kernel may reach another device: no remote copies, remote signals or barrier semaphores. Data moves between devices by JAX's collectives and lax.ppermute only.
A program may use at most 64 MiB of HBM per device.

v0:
```python
import jax
import jax.numpy as jnp
from jax import lax
from jax.sharding import PartitionSpec as P

step_time = 0.1
relax = 0.8
small_suction = 0.04


def with_halo(block, sides, width):
    for axis, dim in sides:
        count = lax.axis_size(axis)
        forward = [(i, i + 1) for i in range(count - 1)]
        backward = [(target, source) for source, target in forward]
        low = lax.ppermute(
            lax.slice_in_dim(block, block.shape[dim] - width, None, axis=dim), axis, forward
        )
        high = lax.ppermute(lax.slice_in_dim(block, 0, width, axis=dim), axis, backward)
        block = jnp.concatenate([low, block, high], axis=dim)
    return block


def soil_fields(soil_type, soil_params):
    fields = []
    for row_id in range(5):
        picked = jnp.zeros(soil_type.shape, jnp.float32)
        for kind_id in range(soil_params.shape[1]):
            picked = jnp.where(soil_type == kind_id, soil_params[row_id, kind_id], picked)
        fields.append(picked)
    return fields


def hydraulics(pressure, params):
    theta_r, theta_s, alpha_vg, shape_n, k_sat = params
    suction = jnp.sqrt(pressure * pressure + small_suction)
    shape_m = 1.0 - 1.0 / shape_n
    power_term = jnp.exp(shape_n * jnp.log(alpha_vg * suction))
    one_plus = 1.0 + power_term
    saturation = jnp.exp(-shape_m * jnp.log(one_plus))
    content = theta_r + (theta_s - theta_r) * saturation
    capacity = (
        (theta_s - theta_r) * shape_m * shape_n * power_term * saturation / (one_plus * suction)
    )
    ratio_term = power_term / one_plus
    conduct = (
        k_sat * jnp.sqrt(saturation) * jnp.square(1.0 - jnp.exp(shape_m * jnp.log(ratio_term)))
    )
    return (content, capacity, conduct)


def fine_balance(padded_head, padded_cond, content, capacity, theta_old, source):
    centre_h = padded_head[1:-1, 1:-1, 1:-1]
    centre_k = padded_cond[1:-1, 1:-1, 1:-1]
    inflow = jnp.zeros_like(centre_h)
    totals = jnp.zeros_like(centre_h)
    for axis_pos in range(3):
        for offset, weight in ((0, 1.0), (2, -1.0)):
            window = [slice(1, -1)] * 3
            window[axis_pos] = slice(offset, offset + centre_h.shape[axis_pos])
            near_h = padded_head[tuple(window)]
            near_k = padded_cond[tuple(window)]
            face_k = jnp.sqrt(centre_k * near_k)
            inflow = inflow + face_k * (near_h - centre_h)
            totals = totals + face_k
            if axis_pos == 0:
                inflow = inflow + weight * face_k
    balance = (content - theta_old) / step_time - inflow - source
    diagonal = capacity / step_time + totals
    return (balance, diagonal)


def coarse_balance(padded_head, padded_trans, storage, base):
    centre_h = padded_head[1:-1, 1:-1]
    centre_t = padded_trans[1:-1, 1:-1]
    inflow = jnp.zeros_like(centre_h)
    totals = jnp.zeros_like(centre_h)
    for axis_pos in range(2):
        for offset in (0, 2):
            window = [slice(1, -1)] * 2
            window[axis_pos] = slice(offset, offset + centre_h.shape[axis_pos])
            face_t = jnp.sqrt(centre_t * padded_trans[tuple(window)])
            inflow = inflow + face_t * (padded_head[tuple(window)] - centre_h)
            totals = totals + face_t
    balance = storage / step_time * (centre_h - base) - inflow
    diagonal = storage / step_time + totals
    return (balance, diagonal)


def coarse_rim_rows(stacked):
    extended = with_halo(stacked, (("area", 1),), 1)
    return jnp.pad(extended, ((0, 0), (0, 0), (1, 1)))


def coarse_cycle(columns, depth_total, rim_rows):
    column_kh = columns[0]
    column_k = columns[1]
    storage = columns[2]
    restricted = columns[3]
    column_rate = columns[4] / depth_total
    base = column_kh / column_k
    padded = rim_rows(jnp.stack([base, column_k]))
    start_flow, start_diag = coarse_balance(padded[0], padded[1], storage, base)
    coarse_rhs = start_flow + restricted
    first = base - relax * (start_flow - coarse_rhs) / start_diag
    transmit = column_k * jnp.exp(column_rate * jnp.tanh(first - base))
    padded = rim_rows(jnp.stack([first, transmit]))
    first_flow, first_diag = coarse_balance(padded[0], padded[1], storage, base)
    second = first - relax * (first_flow - coarse_rhs) / first_diag
    return (base, second)


def shards(pressure, theta_old, source, soil_type, soil_params):
    depth_total = pressure.shape[0] * lax.axis_size("depth")
    params = soil_fields(soil_type, soil_params)
    content, capacity, conduct = hydraulics(pressure, params)
    extended = with_halo(jnp.stack([pressure, conduct]), (("area", 2), ("depth", 1)), 1)
    extended = jnp.pad(extended, ((0, 0), (0, 0), (0, 0), (1, 1)))
    balance, diagonal = fine_balance(extended[0], extended[1], content, capacity, theta_old, source)
    smoothed = pressure - relax * balance / diagonal
    content, capacity, conduct = hydraulics(smoothed, params)
    extended = with_halo(jnp.stack([smoothed, conduct]), (("area", 2), ("depth", 1)), 1)
    extended = jnp.pad(extended, ((0, 0), (0, 0), (0, 0), (1, 1)))
    balance, diagonal = fine_balance(extended[0], extended[1], content, capacity, theta_old, source)
    local_sums = jnp.stack(
        [
            jnp.sum(conduct * smoothed, axis=0),
            jnp.sum(conduct, axis=0),
            jnp.sum(capacity, axis=0),
            -jnp.sum(balance, axis=0),
            jnp.sum(params[2], axis=0),
        ]
    )
    columns = lax.psum(local_sums, "depth")
    base, second = coarse_cycle(columns, depth_total, coarse_rim_rows)
    return (smoothed + (second - base)[None], second)


def solution(mesh):
    in_specs = (
        P("depth", "area", None),
        P("depth", "area", None),
        P("depth", "area", None),
        P("depth", "area", None),
        P(),
    )
    out_specs = (P("depth", "area", None), P("area", None))
    return jax.shard_map(shards, mesh=mesh, in_specs=in_specs, out_specs=out_specs, check_vma=False)
```

profile of v0, /device:TPU:5, one launch (start us, length us, event | category | flops | bytes accessed | tf_op | source)
XLA Modules:
  0.0 171.1 jit_solution(90720884499490197)
XLA Ops:
  7.2 0.0 copy-start
  7.2 0.0 all-reduce.6.cloned.1.call-start
  7.2 2.1 %fusion.109 = (f32[1,1]{1,0:T(1,128)}, f32[1,1]{1,0:T(1,128)}, f32[1,1]{1,0:T(1,128)}, f32[1,1]{1,0:T(1,128)}, f32[1,1]{1,0:T(1,128)}, /*index=5*/f32[1,1]{1,0:T...) fusion(f32[5,12]{1,0:T(8,128)} %param.9), kind=kLoop, calls=%fused_computation.233 | loop fusion | bytes 152 | tf_op jit(solution)/shard_map/slice | solution.py:29
  9.3 2.1 %fusion.108 = (f32[1,1]{1,0:T(1,128)}, f32[1,1]{1,0:T(1,128)}, f32[1,1]{1,0:T(1,128)}, f32[1,1]{1,0:T(1,128)}, f32[1,1]{1,0:T(1,128)}, /*index=5*/f32[1,1]{1,0:T...) fusion(f32[5,12]{1,0:T(8,128)} %param.9), kind=kLoop, calls=%fused_computation.232 | loop fusion | bytes 152 | tf_op jit(solution)/shard_map/slice | solution.py:29
  11.4 1.4 fusion.111
  12.8 9.6 %fusion.105 = (f32[8,1024]{1,0:T(8,128)S(1)}, f32[16,8,1024]{2,1,0:T(8,128)S(1)}, pred[16,8,1024]{2,1,0:T(8,128)(4,1)S(1)}, pred[16,8,1024]{2,1,0:T(8,128)(4,1)S...) fusion(f32[]{:T(128)} %bitcast.47, f32[]{:T(128)} %bitcast.46, ...), kind=kLoop, calls=%fused_computation.231 | loop fusion | flops 3268608 | bytes 2654256 | tf_op jit(solution)/shard_map/reduce_sum | solution.py:131
  22.5 0.0 copy-done
  22.5 0.0 copy-start.4
  22.5 16.5 %fusion.63 = (f32[1,16,8,1024]{3,2,1,0:T(8,128)S(1)}, f32[16,8,1024]{2,1,0:T(8,128)S(1)}, f32[16,8,1024]{2,1,0:T(8,128)S(1)}) fusion(f32[16,8,1024]{2,1,0:T(8,128)S(1)} %get-tuple-element.11, f32[16,8,1024]{2,1,0:T(8,128)S(1)} %copy-done, pred[16,8,1024]{2,1,0:T(8,128)(4,1)S(1)} %get-tuple-element.23, pred[16,8,1024]{2,1,0:T(8,128)(4,1)S(1)} %get-tuple-element.22, ...), kind=kLoop, calls=%fused_computation.123 | loop fusion | flops 5111808 | bytes 4194400 | tf_op jit(solution)/shard_map/stack | solution.py:117
  39.0 0.2 pad_maximum_fusion.11
  39.1 3.7 %collective-permute-start = (f32[2,16,1,1024]{3,2,1,0:T(1,128)S(1)}, f32[2,16,1,1024]{3,2,1,0:T(1,128)S(1)}, u32[]{:S(2)}, u32[]{:S(2)}) collective-permute-start(f32[2,16,1,1024]{3,2,1,0:T(1,128)S(1)} %get-tuple-element.41), channel_id=1, source_target_pairs={{0,2},{2,4},{4,6},{6,8},{8,10},{10,12},{12,14},{14,16},{16,18},{18... | collective-permute-start | bytes 393224 | tf_op jit(solution)/shard_map/ppermute | solution.py:16
  42.8 1.9 %collective-permute-start.1 = (f32[2,16,1,1024]{3,2,1,0:T(1,128)S(1)}, f32[2,16,1,1024]{3,2,1,0:T(1,128)S(1)}, u32[]{:S(2)}, u32[]{:S(2)}) collective-permute-start(f32[2,16,1,1024]{3,2,1,0:T(1,128)S(1)} %get-tuple-element.42), channel_id=1, source_target_pairs={{2,0},{4,2},{6,4},{8,6},{10,8},{12,10},{14,12},{16,14},{18,16},{20... | collective-permute-start | bytes 393224 | tf_op jit(solution)/shard_map/ppermute | solution.py:19
  44.8 0.0 collective-permute-done
  44.8 5.2 %collective-permute-done.1 = f32[2,16,1,1024]{3,2,1,0:T(1,128)S(1)} collective-permute-done((f32[2,16,1,1024]{3,2,1,0:T(1,128)S(1)}, f32[2,16,1,1024]{3,2,1,0:T(1,128)S(1)}, u32[]{:S(2)}, u32[]{:S(2)}) %collective-permute-start.1) | collective-permute-done | bytes 131104 | tf_op jit(solution)/shard_map/ppermute | solution.py:19
  50.1 3.1 %collective-permute-start.2 = (f32[2,1,10,1024]{3,2,1,0:T(8,128)S(1)}, f32[2,1,10,1024]{3,2,1,0:T(8,128)S(1)}, u32[]{:S(2)}, u32[]{:S(2)}) collective-permute-start(f32[2,1,10,1024]{3,2,1,0:T(8,128)S(1)} %get-tuple-element.37), channel_id=1, source_target_pairs={{0,1},{2,3},{4,5},{6,7},{8,9},{10,11},{12,13},{14,15},{16,17},{18,... | collective-permute-start | bytes 245768 | tf_op jit(solution)/shard_map/ppermute | solution.py:16
  53.2 1.3 collective-permute-start.3
  54.5 0.0 copy-done.4
  54.5 0.7 fusion.110
  55.3 0.0 collective-permute-done.2
  55.3 3.7 %collective-permute-done.3 = f32[2,1,10,1024]{3,2,1,0:T(8,128)S(1)} collective-permute-done((f32[2,1,10,1024]{3,2,1,0:T(8,128)S(1)}, f32[2,1,10,1024]{3,2,1,0:T(8,128)S(1)}, u32[]{:S(2)}, u32[]{:S(2)}) %collective-permute-start.3) | collective-permute-done | bytes 81952 | tf_op jit(solution)/shard_map/ppermute | solution.py:19
  58.9 1.5 select_maximum_fusion.5
  60.5 0.0 copy-start.1
  60.5 0.0 copy-start.2
  60.5 0.2 slice_bitcast_fusion.3
  60.7 0.8 copy-done.1
  61.5 0.2 copy-done.2
  61.7 19.8 %fusion.62 = (f32[8,1024]{1,0:T(8,128)S(1)}, f32[16,8,1024]{2,1,0:T(8,128)S(1)}, f32[16,8,1024]{2,1,0:T(8,128)S(1)}) fusion(f32[16,8,1024]{2,1,0:T(8,128)S(1)} %get-tuple-element.29, pred[16,8,1024]{2,1,0:T(8,128)(4,1)S(1)} %get-tuple-element.23, pred[16,8,1024]{2,1,0:T(8,128)(4,1)S(1)} %get-tuple-element.22, ...), kind=kLoop, calls=%fused_computation.122 | loop fusion | flops 12181504 | bytes 12615776 | tf_op jit(solution)/shard_map/reduce_sum | solution.py:129
  81.5 0.6 fusion.101
  82.1 0.2 pad_maximum_fusion.5
  82.3 4.2 %collective-permute-start.4 = (f32[2,16,1,1024]{3,2,1,0:T(1,128)S(1)}, f32[2,16,1,1024]{3,2,1,0:T(1,128)S(1)}, u32[]{:S(2)}, u32[]{:S(2)}) collective-permute-start(f32[2,16,1,1024]{3,2,1,0:T(1,128)S(1)} %get-tuple-element.39), channel_id=1, source_target_pairs={{0,2},{2,4},{4,6},{6,8},{8,10},{10,12},{12,14},{14,16},{16,18},{18... | collective-permute-start | bytes 393224 | tf_op jit(solution)/shard_map/ppermute | solution.py:16
  86.5 1.9 %collective-permute-start.5 = (f32[2,16,1,1024]{3,2,1,0:T(1,128)S(1)}, f32[2,16,1,1024]{3,2,1,0:T(1,128)S(1)}, u32[]{:S(2)}, u32[]{:S(2)}) collective-permute-start(f32[2,16,1,1024]{3,2,1,0:T(1,128)S(1)} %get-tuple-element.40), channel_id=1, source_target_pairs={{2,0},{4,2},{6,4},{8,6},{10,8},{12,10},{14,12},{16,14},{18,16},{20... | collective-permute-start | bytes 393224 | tf_op jit(solution)/shard_map/ppermute | solution.py:19
  88.5 0.0 collective-permute-done.4
  88.5 5.2 %collective-permute-done.5 = f32[2,16,1,1024]{3,2,1,0:T(1,128)S(1)} collective-permute-done((f32[2,16,1,1024]{3,2,1,0:T(1,128)S(1)}, f32[2,16,1,1024]{3,2,1,0:T(1,128)S(1)}, u32[]{:S(2)}, u32[]{:S(2)}) %collective-permute-start.5) | collective-permute-done | bytes 131104 | tf_op jit(solution)/shard_map/ppermute | solution.py:19
  93.7 1.3 collective-permute-start.6
  95.1 1.5 collective-permute-start.7
  96.5 0.4 collective-permute-done.6
  97.0 3.8 %collective-permute-done.7 = f32[2,1,10,1024]{3,2,1,0:T(8,128)S(1)} collective-permute-done((f32[2,1,10,1024]{3,2,1,0:T(8,128)S(1)}, f32[2,1,10,1024]{3,2,1,0:T(8,128)S(1)}, u32[]{:S(2)}, u32[]{:S(2)}) %collective-permute-start.7) | collective-permute-done | bytes 81952 | tf_op jit(solution)/shard_map/ppermute | solution.py:19
  100.8 1.5 select_maximum_fusion
  102.3 0.2 slice_bitcast_fusion.1
  102.5 18.4 %fusion.64 = f32[8,1024]{1,0:T(8,128)S(1)} fusion(f32[16,8,1024]{2,1,0:T(8,128)S(1)} %copy-done.1, f32[18,10,1026]{2,1,0:T(8,128)S(1)} %get-tuple-element.32, f32[18,10,1026]{2,1,0:T(8,128)S(1)} %get-tuple-element.31, f32[16,8,1024]{2,1,0:T(8,128)S(1)} %copy-done.2, f32[16,8,1024]{2,1,0:T(8,128)S(1)} %get-tuple-element.25, ...), kind=kLoop, calls=%fused_computation.124 | loop fusion | flops 8249344 | bytes 11042912 | tf_op jit(solution)/shard_map/reduce_sum | solution.py:130
  120.9 0.0 copy-start.3
  120.9 0.7 copy-done.3
  121.6 0.0 all-reduce.6.cloned.1.call-update
  121.6 20.4 %all-reduce.6.cloned.1.call-done = f32[5,8,1024]{2,1,0:T(8,128)} async-done(((f32[5,8,1024]{2,1,0:T(8,128)}), f32[5,8,1024]{2,1,0:T(8,128)}) %all-reduce.6.cloned.1.call-update) | async-done | bytes 163856 | tf_op jit(solution)/shard_map/psum | solution.py:134
  141.9 0.8 slice_divide_fusion
  142.8 4.1 %collective-permute-start.8 = (f32[2,1,1024]{2,1,0:T(1,128)S(1)}, f32[2,1,1024]{2,1,0:T(1,128)S(1)}, u32[]{:S(2)}, u32[]{:S(2)}) collective-permute-start(f32[2,1,1024]{2,1,0:T(1,128)S(1)} %get-tuple-element.51), channel_id=1, source_target_pairs={{0,2},{2,4},{4,6},{6,8},{8,10},{10,12},{12,14},{14,16},{16,18},{18... | collective-permute-start | bytes 24584 | tf_op jit(solution)/shard_map/ppermute | solution.py:16
  146.9 1.9 %collective-permute-start.9 = (f32[2,1,1024]{2,1,0:T(1,128)S(1)}, f32[2,1,1024]{2,1,0:T(1,128)S(1)}, u32[]{:S(2)}, u32[]{:S(2)}) collective-permute-start(f32[2,1,1024]{2,1,0:T(1,128)S(1)} %get-tuple-element.52), channel_id=1, source_target_pairs={{2,0},{4,2},{6,4},{8,6},{10,8},{12,10},{14,12},{16,14},{18,16},{20... | collective-permute-start | bytes 24584 | tf_op jit(solution)/shard_map/ppermute | solution.py:19
  148.8 0.0 collective-permute-done.8
  148.8 3.9 %collective-permute-done.9 = f32[2,1,1024]{2,1,0:T(1,128)S(1)} collective-permute-done((f32[2,1,1024]{2,1,0:T(1,128)S(1)}, f32[2,1,1024]{2,1,0:T(1,128)S(1)}, u32[]{:S(2)}, u32[]{:S(2)}) %collective-permute-start.9) | collective-permute-done | bytes 8224 | tf_op jit(solution)/shard_map/ppermute | solution.py:19
  152.7 0.1 select_maximum_fusion.13
  152.9 1.0 fusion.86
  153.9 1.9 %collective-permute-start.10 = (f32[2,1,1024]{2,1,0:T(1,128)S(1)}, f32[2,1,1024]{2,1,0:T(1,128)S(1)}, u32[]{:S(2)}, u32[]{:S(2)}) collective-permute-start(f32[2,1,1024]{2,1,0:T(1,128)S(1)} %get-tuple-element.49), channel_id=1, source_target_pairs={{0,2},{2,4},{4,6},{6,8},{8,10},{10,12},{12,14},{14,16},{16,18},{18... | collective-permute-start | bytes 24584 | tf_op jit(solution)/shard_map/ppermute | solution.py:16
  155.9 2.4 %collective-permute-start.11 = (f32[2,1,1024]{2,1,0:T(1,128)S(1)}, f32[2,1,1024]{2,1,0:T(1,128)S(1)}, u32[]{:S(2)}, u32[]{:S(2)}) collective-permute-start(f32[2,1,1024]{2,1,0:T(1,128)S(1)} %get-tuple-element.50), channel_id=1, source_target_pairs={{2,0},{4,2},{6,4},{8,6},{10,8},{12,10},{14,12},{16,14},{18,16},{20... | collective-permute-start | bytes 24584 | tf_op jit(solution)/shard_map/ppermute | solution.py:19
  158.3 0.0 collective-permute-done.10
  158.3 3.5 %collective-permute-done.11 = f32[2,1,1024]{2,1,0:T(1,128)S(1)} collective-permute-done((f32[2,1,1024]{2,1,0:T(1,128)S(1)}, f32[2,1,1024]{2,1,0:T(1,128)S(1)}, u32[]{:S(2)}, u32[]{:S(2)}) %collective-permute-start.11) | collective-permute-done | bytes 8224 | tf_op jit(solution)/shard_map/ppermute | solution.py:19
  161.7 0.1 select_maximum_fusion.10
  161.9 1.5 fusion.102
  163.5 0.8 broadcast_add_fusion
  (11 shorter events, 0.2 us)
Async XLA Ops:
  7.2 15.3 %copy-start = (f32[16,8,1024]{2,1,0:T(8,128)S(1)}, f32[16,8,1024]{2,1,0:T(8,128)}, u32[]{:S(2)}) copy-start(f32[16,8,1024]{2,1,0:T(8,128)} %param.5) | copy-start | bytes 1572868
  7.2 134.8 %all-reduce.6.cloned.1.call-start = ((), (), s32[]{:S(2)}) async-start(), calls=%async_computation | async-start | bytes 327680 | tf_op jit(solution)/shard_map/psum | solution.py:134
  22.5 32.0 %copy-start.4 = (f32[5,12]{1,0:T(8,128)S(1)}, f32[5,12]{1,0:T(8,128)}, u32[]{:S(2)}) copy-start(f32[5,12]{1,0:T(8,128)} %param.9) | copy-start | bytes 724
  39.1 5.6 %collective-permute-start = (f32[2,16,1,1024]{3,2,1,0:T(1,128)S(1)}, f32[2,16,1,1024]{3,2,1,0:T(1,128)S(1)}, u32[]{:S(2)}, u32[]{:S(2)}) collective-permute-start(f32[2,16,1,1024]{3,2,1,0:T(1,128)S(1)} %get-tuple-element.41), channel_id=1, source_target_pairs={{0,2},{2,4},{4,6},{6,8},{8,10},{10,12},{12,14},{14,16},{16,18},{18... | collective-permute-start | bytes 393224 | tf_op jit(solution)/shard_map/ppermute | solution.py:16
  42.8 7.2 %collective-permute-start.1 = (f32[2,16,1,1024]{3,2,1,0:T(1,128)S(1)}, f32[2,16,1,1024]{3,2,1,0:T(1,128)S(1)}, u32[]{:S(2)}, u32[]{:S(2)}) collective-permute-start(f32[2,16,1,1024]{3,2,1,0:T(1,128)S(1)} %get-tuple-element.42), channel_id=1, source_target_pairs={{2,0},{4,2},{6,4},{8,6},{10,8},{12,10},{14,12},{16,14},{18,16},{20... | collective-permute-start | bytes 393224 | tf_op jit(solution)/shard_map/ppermute | solution.py:19
  50.1 5.2 %collective-permute-start.2 = (f32[2,1,10,1024]{3,2,1,0:T(8,128)S(1)}, f32[2,1,10,1024]{3,2,1,0:T(8,128)S(1)}, u32[]{:S(2)}, u32[]{:S(2)}) collective-permute-start(f32[2,1,10,1024]{3,2,1,0:T(8,128)S(1)} %get-tuple-element.37), channel_id=1, source_target_pairs={{0,1},{2,3},{4,5},{6,7},{8,9},{10,11},{12,13},{14,15},{16,17},{18,... | collective-permute-start | bytes 245768 | tf_op jit(solution)/shard_map/ppermute | solution.py:16
  53.2 5.7 %collective-permute-start.3 = (f32[2,1,10,1024]{3,2,1,0:T(8,128)S(1)}, f32[2,1,10,1024]{3,2,1,0:T(8,128)S(1)}, u32[]{:S(2)}, u32[]{:S(2)}) collective-permute-start(f32[2,1,10,1024]{3,2,1,0:T(8,128)S(1)} %get-tuple-element.38), channel_id=1, source_target_pairs={{1,0},{3,2},{5,4},{7,6},{9,8},{11,10},{13,12},{15,14},{17,16},{19,... | collective-permute-start | bytes 245768 | tf_op jit(solution)/shard_map/ppermute | solution.py:19
  60.5 1.0 copy-start.1
  60.5 1.2 copy-start.2
  82.3 6.2 %collective-permute-start.4 = (f32[2,16,1,1024]{3,2,1,0:T(1,128)S(1)}, f32[2,16,1,1024]{3,2,1,0:T(1,128)S(1)}, u32[]{:S(2)}, u32[]{:S(2)}) collective-permute-start(f32[2,16,1,1024]{3,2,1,0:T(1,128)S(1)} %get-tuple-element.39), channel_id=1, source_target_pairs={{0,2},{2,4},{4,6},{6,8},{8,10},{10,12},{12,14},{14,16},{16,18},{18... | collective-permute-start | bytes 393224 | tf_op jit(solution)/shard_map/ppermute | solution.py:16
  86.5 7.2 %collective-permute-start.5 = (f32[2,16,1,1024]{3,2,1,0:T(1,128)S(1)}, f32[2,16,1,1024]{3,2,1,0:T(1,128)S(1)}, u32[]{:S(2)}, u32[]{:S(2)}) collective-permute-start(f32[2,16,1,1024]{3,2,1,0:T(1,128)S(1)} %get-tuple-element.40), channel_id=1, source_target_pairs={{2,0},{4,2},{6,4},{8,6},{10,8},{12,10},{14,12},{16,14},{18,16},{20... | collective-permute-start | bytes 393224 | tf_op jit(solution)/shard_map/ppermute | solution.py:19
  93.7 3.2 %collective-permute-start.6 = (f32[2,1,10,1024]{3,2,1,0:T(8,128)S(1)}, f32[2,1,10,1024]{3,2,1,0:T(8,128)S(1)}, u32[]{:S(2)}, u32[]{:S(2)}) collective-permute-start(f32[2,1,10,1024]{3,2,1,0:T(8,128)S(1)} %get-tuple-element.35), channel_id=1, source_target_pairs={{0,1},{2,3},{4,5},{6,7},{8,9},{10,11},{12,13},{14,15},{16,17},{18,... | collective-permute-start | bytes 245768 | tf_op jit(solution)/shard_map/ppermute | solution.py:16
  95.1 5.7 %collective-permute-start.7 = (f32[2,1,10,1024]{3,2,1,0:T(8,128)S(1)}, f32[2,1,10,1024]{3,2,1,0:T(8,128)S(1)}, u32[]{:S(2)}, u32[]{:S(2)}) collective-permute-start(f32[2,1,10,1024]{3,2,1,0:T(8,128)S(1)} %get-tuple-element.36), channel_id=1, source_target_pairs={{1,0},{3,2},{5,4},{7,6},{9,8},{11,10},{13,12},{15,14},{17,16},{19,... | collective-permute-start | bytes 245768 | tf_op jit(solution)/shard_map/ppermute | solution.py:19
  120.9 0.7 copy-start.3
  142.8 6.0 %collective-permute-start.8 = (f32[2,1,1024]{2,1,0:T(1,128)S(1)}, f32[2,1,1024]{2,1,0:T(1,128)S(1)}, u32[]{:S(2)}, u32[]{:S(2)}) collective-permute-start(f32[2,1,1024]{2,1,0:T(1,128)S(1)} %get-tuple-element.51), channel_id=1, source_target_pairs={{0,2},{2,4},{4,6},{6,8},{8,10},{10,12},{12,14},{14,16},{16,18},{18... | collective-permute-start | bytes 24584 | tf_op jit(solution)/shard_map/ppermute | solution.py:16
  146.9 5.9 %collective-permute-start.9 = (f32[2,1,1024]{2,1,0:T(1,128)S(1)}, f32[2,1,1024]{2,1,0:T(1,128)S(1)}, u32[]{:S(2)}, u32[]{:S(2)}) collective-permute-start(f32[2,1,1024]{2,1,0:T(1,128)S(1)} %get-tuple-element.52), channel_id=1, source_target_pairs={{2,0},{4,2},{6,4},{8,6},{10,8},{12,10},{14,12},{16,14},{18,16},{20... | collective-permute-start | bytes 24584 | tf_op jit(solution)/shard_map/ppermute | solution.py:19
  153.9 4.3 %collective-permute-start.10 = (f32[2,1,1024]{2,1,0:T(1,128)S(1)}, f32[2,1,1024]{2,1,0:T(1,128)S(1)}, u32[]{:S(2)}, u32[]{:S(2)}) collective-permute-start(f32[2,1,1024]{2,1,0:T(1,128)S(1)} %get-tuple-element.49), channel_id=1, source_target_pairs={{0,2},{2,4},{4,6},{6,8},{8,10},{10,12},{12,14},{14,16},{16,18},{18... | collective-permute-start | bytes 24584 | tf_op jit(solution)/shard_map/ppermute | solution.py:16
  155.9 5.9 %collective-permute-start.11 = (f32[2,1,1024]{2,1,0:T(1,128)S(1)}, f32[2,1,1024]{2,1,0:T(1,128)S(1)}, u32[]{:S(2)}, u32[]{:S(2)}) collective-permute-start(f32[2,1,1024]{2,1,0:T(1,128)S(1)} %get-tuple-element.50), channel_id=1, source_target_pairs={{2,0},{4,2},{6,4},{8,6},{10,8},{12,10},{14,12},{16,14},{18,16},{20... | collective-permute-start | bytes 24584 | tf_op jit(solution)/shard_map/ppermute | solution.py:19
Sparse Core Ops, SparseCore 0:
  121.7 20.1 all-reduce.5
where the time goes:
time: 173 us; the launch traced here: 171 us
  other arithmetic  72.9 us (42%)
  waiting for transfers between devices  46.1 us (27%)
  starting transfers between devices  29.4 us (17%)
  between operations  14.4 us (8%)
  local copies, waits for them, and re-layouts  8.38 us (5%)
    ppermute x6, waiting for transfers between devices, with_halo(): lax.ppermute(lax.slice_in_dim(block, 0, width, axis=dim), axis, backward)  25.3 us
    psum x1, waiting for transfers between devices, shards(): columns = lax.psum(local_sums, 'depth')  20.4 us
    reduce_sum x1, other arithmetic, shards(): jnp.sum(capacity, axis=0)  19.8 us
    ppermute x6, starting transfers between devices, with_halo(): lax.ppermute(lax.slice_in_dim(block, block.shape[dim] - width, None, axis...  18.4 us
    reduce_sum x1, other arithmetic, shards(): jnp.sum(balance, axis=0)  18.4 us
    another operation x1, other arithmetic, shards(): jnp.stack([pressure, conduct])  16.5 us
    ppermute x6, starting transfers between devices, with_halo(): lax.ppermute(lax.slice_in_dim(block, 0, width, axis=dim), axis, backward)  10.9 us
    reduce_sum x1, other arithmetic, shards(): jnp.sum(params[2], axis=0)  9.63 us
  transfers between devices with their start and end apart: 13, of which 8 were waited for; matrix products, arithmetic and copies ran while one was open for 0% of the time, Pallas kernels for 0%

commit v1 on v0

--- a/solution.py
+++ b/solution.py
@@ -131,7 +131,12 @@
             jnp.sum(params[2], axis=0),
         ]
     )
-    columns = lax.psum(local_sums, "depth")
+
+    def plan_lines(message):
+        built = jax.lax.all_gather(message, axis_name="depth").sum(axis=0)
+        return built
+
+    columns = plan_lines(local_sums)
     base, second = coarse_cycle(columns, depth_total, coarse_rim_rows)
     return (smoothed + (second - base)[None], second)
 

time: 173 us -> 141 us (0.82)
  waiting for transfers between devices: 46.1 us -> 25.8 us
  between operations: 14.4 us -> 1 us
  blocking collectives: 0 us -> 4.85 us
  other arithmetic: 72.9 us -> 70.7 us
    psum x1 -> x0, waiting for transfers between devices: 20.4 us -> none  [shards(): columns = lax.psum(local_sums, 'depth')]
    all_gather x0 -> x1, blocking collectives: none -> 4.85 us  [plan_lines(): built = jax.lax.all_gather(message, axis_name='depth').sum(axis=0)]
  transfers between devices with their start and end apart: 13 -> 12, of which waited for: 8 -> 7; matrix products, arithmetic and copies ran while one was open for 0% -> 1% of each run, Pallas kernels for 0% -> 0%
where the time goes in v1:
time: 141 us; the launch traced here: 139 us
  other arithmetic  70.7 us (50%)
  starting transfers between devices  29.4 us (21%)
  waiting for transfers between devices  25.8 us (18%)
  local copies, waits for them, and re-layouts  7.75 us (5%)
  blocking collectives  4.85 us (3%)
    ppermute x6, waiting for transfers between devices, with_halo(): lax.ppermute(lax.slice_in_dim(block, 0, width, axis=dim), axis, backward)  25.3 us
    reduce_sum x1, other arithmetic, shards(): jnp.sum(capacity, axis=0)  19.9 us
    ppermute x6, starting transfers between devices, with_halo(): lax.ppermute(lax.slice_in_dim(block, block.shape[dim] - width, None, axis...  18.5 us
    reduce_sum x1, other arithmetic, shards(): jnp.sum(balance, axis=0)  18.4 us
    another operation x1, other arithmetic, shards(): jnp.stack([pressure, conduct])  16.5 us
    ppermute x6, starting transfers between devices, with_halo(): lax.ppermute(lax.slice_in_dim(block, 0, width, axis=dim), axis, backward)  10.9 us
    reduce_sum x1, other arithmetic, shards(): jnp.sum(params[2], axis=0)  9.67 us
    slice x4, local copies, waits for them, and re-layouts, soil_fields(): soil_params[row_id, kind_id]  6.34 us
  transfers between devices with their start and end apart: 12, of which 7 were waited for; matrix products, arithmetic and copies ran while one was open for 1% of the time, Pallas kernels for 0%

profile of v1, /device:TPU:5, one launch (start us, length us, event | category | flops | bytes accessed | tf_op | source)
XLA Modules:
  0.0 139.5 jit_solution(2432604296362628139)
XLA Ops:
  0.6 0.0 copy-start
  0.6 2.1 %fusion.109 = (f32[1,1]{1,0:T(1,128)}, f32[1,1]{1,0:T(1,128)}, f32[1,1]{1,0:T(1,128)}, f32[1,1]{1,0:T(1,128)}, f32[1,1]{1,0:T(1,128)}, /*index=5*/f32[1,1]{1,0:T...) fusion(f32[5,12]{1,0:T(8,128)} %param.9), kind=kLoop, calls=%fused_computation.233 | loop fusion | bytes 152 | tf_op jit(solution)/shard_map/slice | solution.py:29
  2.7 2.1 %fusion.108 = (f32[1,1]{1,0:T(1,128)}, f32[1,1]{1,0:T(1,128)}, f32[1,1]{1,0:T(1,128)}, f32[1,1]{1,0:T(1,128)}, f32[1,1]{1,0:T(1,128)}, /*index=5*/f32[1,1]{1,0:T...) fusion(f32[5,12]{1,0:T(8,128)} %param.9), kind=kLoop, calls=%fused_computation.232 | loop fusion | bytes 152 | tf_op jit(solution)/shard_map/slice | solution.py:29
  4.8 1.4 %fusion.111 = (f32[1,1]{1,0:T(1,128)}, f32[1,1]{1,0:T(1,128)}, f32[1,1]{1,0:T(1,128)}) fusion(f32[5,12]{1,0:T(8,128)} %param.9), kind=kLoop, calls=%fused_computation.235 | loop fusion | bytes 24 | tf_op jit(solution)/shard_map/slice | solution.py:29
  6.3 9.7 %fusion.105 = (f32[8,1024]{1,0:T(8,128)S(1)}, f32[16,8,1024]{2,1,0:T(8,128)S(1)}, pred[16,8,1024]{2,1,0:T(8,128)(4,1)S(1)}, pred[16,8,1024]{2,1,0:T(8,128)(4,1)S...) fusion(f32[]{:T(128)} %bitcast.47, f32[]{:T(128)} %bitcast.46, ...), kind=kLoop, calls=%fused_computation.231 | loop fusion | flops 3268608 | bytes 2654256 | tf_op jit(solution)/shard_map/reduce_sum | solution.py:131
  15.9 0.0 copy-done
  15.9 0.0 copy-start.3
  16.0 16.5 %fusion.63 = (f32[1,16,8,1024]{3,2,1,0:T(8,128)S(1)}, f32[16,8,1024]{2,1,0:T(8,128)S(1)}, f32[16,8,1024]{2,1,0:T(8,128)S(1)}) fusion(f32[16,8,1024]{2,1,0:T(8,128)S(1)} %get-tuple-element.11, f32[16,8,1024]{2,1,0:T(8,128)S(1)} %copy-done, pred[16,8,1024]{2,1,0:T(8,128)(4,1)S(1)} %get-tuple-element.23, pred[16,8,1024]{2,1,0:T(8,128)(4,1)S(1)} %get-tuple-element.22, ...), kind=kLoop, calls=%fused_computation.123 | loop fusion | flops 5111808 | bytes 4194400 | tf_op jit(solution)/shard_map/stack | solution.py:117
  32.5 0.2 pad_maximum_fusion.11
  32.7 3.7 %collective-permute-start = (f32[2,16,1,1024]{3,2,1,0:T(1,128)S(1)}, f32[2,16,1,1024]{3,2,1,0:T(1,128)S(1)}, u32[]{:S(2)}, u32[]{:S(2)}) collective-permute-start(f32[2,16,1,1024]{3,2,1,0:T(1,128)S(1)} %get-tuple-element.41), channel_id=1, source_target_pairs={{0,2},{2,4},{4,6},{6,8},{8,10},{10,12},{12,14},{14,16},{16,18},{18... | collective-permute-start | bytes 393224 | tf_op jit(solution)/shard_map/ppermute | solution.py:16
  36.4 1.9 %collective-permute-start.1 = (f32[2,16,1,1024]{3,2,1,0:T(1,128)S(1)}, f32[2,16,1,1024]{3,2,1,0:T(1,128)S(1)}, u32[]{:S(2)}, u32[]{:S(2)}) collective-permute-start(f32[2,16,1,1024]{3,2,1,0:T(1,128)S(1)} %get-tuple-element.42), channel_id=1, source_target_pairs={{2,0},{4,2},{6,4},{8,6},{10,8},{12,10},{14,12},{16,14},{18,16},{20... | collective-permute-start | bytes 393224 | tf_op jit(solution)/shard_map/ppermute | solution.py:19
  38.3 0.0 collective-permute-done
  38.3 5.2 %collective-permute-done.1 = f32[2,16,1,1024]{3,2,1,0:T(1,128)S(1)} collective-permute-done((f32[2,16,1,1024]{3,2,1,0:T(1,128)S(1)}, f32[2,16,1,1024]{3,2,1,0:T(1,128)S(1)}, u32[]{:S(2)}, u32[]{:S(2)}) %collective-permute-start.1) | collective-permute-done | bytes 131104 | tf_op jit(solution)/shard_map/ppermute | solution.py:19
  43.6 3.1 %collective-permute-start.2 = (f32[2,1,10,1024]{3,2,1,0:T(8,128)S(1)}, f32[2,1,10,1024]{3,2,1,0:T(8,128)S(1)}, u32[]{:S(2)}, u32[]{:S(2)}) collective-permute-start(f32[2,1,10,1024]{3,2,1,0:T(8,128)S(1)} %get-tuple-element.37), channel_id=1, source_target_pairs={{0,1},{2,3},{4,5},{6,7},{8,9},{10,11},{12,13},{14,15},{16,17},{18,... | collective-permute-start | bytes 245768 | tf_op jit(solution)/shard_map/ppermute | solution.py:16
  46.7 1.3 collective-permute-start.3
  48.0 0.0 copy-done.3
  48.1 0.7 fusion.110
  48.8 0.0 collective-permute-done.2
  48.8 3.7 %collective-permute-done.3 = f32[2,1,10,1024]{3,2,1,0:T(8,128)S(1)} collective-permute-done((f32[2,1,10,1024]{3,2,1,0:T(8,128)S(1)}, f32[2,1,10,1024]{3,2,1,0:T(8,128)S(1)}, u32[]{:S(2)}, u32[]{:S(2)}) %collective-permute-start.3) | collective-permute-done | bytes 81952 | tf_op jit(solution)/shard_map/ppermute | solution.py:19
  52.5 1.6 %select_maximum_fusion.5 = f32[2,18,10,1026]{3,2,1,0:T(8,128)S(1)} fusion(f32[2,1,10,1024]{3,2,1,0:T(8,128)S(1)} %collective-permute-done.3, f32[2,1,10,1024]{3,2,1,0:T(8,128)S(1)} %collective-permute-done.2, f32[2,16,1,1024]{3,2,1,0:T(1,128)S(1)} %collective-permute-done.1, f32[2,16,1,1024]{3,2,1,0:T(1,128)S(1)} %collective-permute-done, ...), kind=kLoop, calls=%fused_computation.7 | loop fusion | flops 5171040 | bytes 2952000 | tf_op jit(solution)/shard_map/concatenate | solution.py:20
  54.0 0.0 copy-start.1
  54.0 0.0 copy-start.2
  54.0 0.2 slice_bitcast_fusion.3
  54.2 0.8 copy-done.1
  55.1 0.2 copy-done.2
  55.2 19.9 %fusion.62 = (f32[8,1024]{1,0:T(8,128)S(1)}, f32[16,8,1024]{2,1,0:T(8,128)S(1)}, f32[16,8,1024]{2,1,0:T(8,128)S(1)}) fusion(f32[16,8,1024]{2,1,0:T(8,128)S(1)} %get-tuple-element.29, pred[16,8,1024]{2,1,0:T(8,128)(4,1)S(1)} %get-tuple-element.23, pred[16,8,1024]{2,1,0:T(8,128)(4,1)S(1)} %get-tuple-element.22, ...), kind=kLoop, calls=%fused_computation.122 | loop fusion | flops 12181504 | bytes 12615776 | tf_op jit(solution)/shard_map/reduce_sum | solution.py:129
  75.1 0.6 fusion.101
  75.7 0.2 pad_maximum_fusion.5
  75.8 4.2 %collective-permute-start.4 = (f32[2,16,1,1024]{3,2,1,0:T(1,128)S(1)}, f32[2,16,1,1024]{3,2,1,0:T(1,128)S(1)}, u32[]{:S(2)}, u32[]{:S(2)}) collective-permute-start(f32[2,16,1,1024]{3,2,1,0:T(1,128)S(1)} %get-tuple-element.39), channel_id=1, source_target_pairs={{0,2},{2,4},{4,6},{6,8},{8,10},{10,12},{12,14},{14,16},{16,18},{18... | collective-permute-start | bytes 393224 | tf_op jit(solution)/shard_map/ppermute | solution.py:16
  80.1 1.9 %collective-permute-start.5 = (f32[2,16,1,1024]{3,2,1,0:T(1,128)S(1)}, f32[2,16,1,1024]{3,2,1,0:T(1,128)S(1)}, u32[]{:S(2)}, u32[]{:S(2)}) collective-permute-start(f32[2,16,1,1024]{3,2,1,0:T(1,128)S(1)} %get-tuple-element.40), channel_id=1, source_target_pairs={{2,0},{4,2},{6,4},{8,6},{10,8},{12,10},{14,12},{16,14},{18,16},{20... | collective-permute-start | bytes 393224 | tf_op jit(solution)/shard_map/ppermute | solution.py:19
  82.0 0.0 collective-permute-done.4
  82.0 5.2 %collective-permute-done.5 = f32[2,16,1,1024]{3,2,1,0:T(1,128)S(1)} collective-permute-done((f32[2,16,1,1024]{3,2,1,0:T(1,128)S(1)}, f32[2,16,1,1024]{3,2,1,0:T(1,128)S(1)}, u32[]{:S(2)}, u32[]{:S(2)}) %collective-permute-start.5) | collective-permute-done | bytes 131104 | tf_op jit(solution)/shard_map/ppermute | solution.py:19
  87.3 1.3 collective-permute-start.6
  88.6 1.5 %collective-permute-start.7 = (f32[2,1,10,1024]{3,2,1,0:T(8,128)S(1)}, f32[2,1,10,1024]{3,2,1,0:T(8,128)S(1)}, u32[]{:S(2)}, u32[]{:S(2)}) collective-permute-start(f32[2,1,10,1024]{3,2,1,0:T(8,128)S(1)} %get-tuple-element.36), channel_id=1, source_target_pairs={{1,0},{3,2},{5,4},{7,6},{9,8},{11,10},{13,12},{15,14},{17,16},{19,... | collective-permute-start | bytes 245768 | tf_op jit(solution)/shard_map/ppermute | solution.py:19
  90.1 0.4 collective-permute-done.6
  90.6 3.8 %collective-permute-done.7 = f32[2,1,10,1024]{3,2,1,0:T(8,128)S(1)} collective-permute-done((f32[2,1,10,1024]{3,2,1,0:T(8,128)S(1)}, f32[2,1,10,1024]{3,2,1,0:T(8,128)S(1)}, u32[]{:S(2)}, u32[]{:S(2)}) %collective-permute-start.7) | collective-permute-done | bytes 81952 | tf_op jit(solution)/shard_map/ppermute | solution.py:19
  94.3 1.5 %select_maximum_fusion = f32[2,18,10,1026]{3,2,1,0:T(8,128)S(1)} fusion(f32[2,1,10,1024]{3,2,1,0:T(8,128)S(1)} %collective-permute-done.7, f32[2,1,10,1024]{3,2,1,0:T(8,128)S(1)} %collective-permute-done.6, f32[2,16,1,1024]{3,2,1,0:T(1,128)S(1)} %collective-permute-done.5, f32[2,16,1,1024]{3,2,1,0:T(1,128)S(1)} %collective-permute-done.4, ...), kind=kLoop, calls=%fused_computation.2 | loop fusion | flops 5171040 | bytes 2952000 | tf_op jit(solution)/shard_map/concatenate | solution.py:20
  95.9 0.2 slice_bitcast_fusion.1
  96.1 18.4 %fusion.64 = f32[8,1024]{1,0:T(8,128)S(1)} fusion(f32[16,8,1024]{2,1,0:T(8,128)S(1)} %copy-done.1, f32[18,10,1026]{2,1,0:T(8,128)S(1)} %get-tuple-element.32, f32[18,10,1026]{2,1,0:T(8,128)S(1)} %get-tuple-element.31, f32[16,8,1024]{2,1,0:T(8,128)S(1)} %copy-done.2, f32[16,8,1024]{2,1,0:T(8,128)S(1)} %get-tuple-element.25, ...), kind=kLoop, calls=%fused_computation.124 | loop fusion | flops 8249344 | bytes 11042912 | tf_op jit(solution)/shard_map/reduce_sum | solution.py:130
  114.5 4.8 %all-gather = f32[10,8,1024]{2,1,0:T(8,128)S(1)} all-gather(f32[5,8,1024]{2,1,0:T(8,128)S(1)} %bitcast_dynamic-update-slice_fusion), channel_id=2, replica_groups=mesh['area'=16,'depth'=2] {'depth'}, dimensions={0}, use_global_device_ids=true | all-gather | bytes 491520 | tf_op jit(solution)/shard_map/all_gather | solution.py:136
  119.4 4.2 %collective-permute-start.8 = (f32[2,1,1024]{2,1,0:T(1,128)S(1)}, f32[2,1,1024]{2,1,0:T(1,128)S(1)}, u32[]{:S(2)}, u32[]{:S(2)}) collective-permute-start(f32[2,1,1024]{2,1,0:T(1,128)S(1)} %get-tuple-element.51), channel_id=1, source_target_pairs={{0,2},{2,4},{4,6},{6,8},{8,10},{10,12},{12,14},{14,16},{16,18},{18... | collective-permute-start | bytes 24584 | tf_op jit(solution)/shard_map/ppermute | solution.py:16
  123.7 1.9 %collective-permute-start.9 = (f32[2,1,1024]{2,1,0:T(1,128)S(1)}, f32[2,1,1024]{2,1,0:T(1,128)S(1)}, u32[]{:S(2)}, u32[]{:S(2)}) collective-permute-start(f32[2,1,1024]{2,1,0:T(1,128)S(1)} %get-tuple-element.52), channel_id=1, source_target_pairs={{2,0},{4,2},{6,4},{8,6},{10,8},{12,10},{14,12},{16,14},{18,16},{20... | collective-permute-start | bytes 24584 | tf_op jit(solution)/shard_map/ppermute | solution.py:19
  125.6 0.0 collective-permute-done.8
  125.6 3.9 %collective-permute-done.9 = f32[2,1,1024]{2,1,0:T(1,128)S(1)} collective-permute-done((f32[2,1,1024]{2,1,0:T(1,128)S(1)}, f32[2,1,1024]{2,1,0:T(1,128)S(1)}, u32[]{:S(2)}, u32[]{:S(2)}) %collective-permute-start.9) | collective-permute-done | bytes 8224 | tf_op jit(solution)/shard_map/ppermute | solution.py:19
  129.5 0.1 select_maximum_fusion.13
  129.7 0.2 fusion.86
  129.9 1.9 %collective-permute-start.10 = (f32[2,1,1024]{2,1,0:T(1,128)S(1)}, f32[2,1,1024]{2,1,0:T(1,128)S(1)}, u32[]{:S(2)}, u32[]{:S(2)}) collective-permute-start(f32[2,1,1024]{2,1,0:T(1,128)S(1)} %get-tuple-element.49), channel_id=1, source_target_pairs={{0,2},{2,4},{4,6},{6,8},{8,10},{10,12},{12,14},{14,16},{16,18},{18... | collective-permute-start | bytes 24584 | tf_op jit(solution)/shard_map/ppermute | solution.py:16
  131.9 2.4 %collective-permute-start.11 = (f32[2,1,1024]{2,1,0:T(1,128)S(1)}, f32[2,1,1024]{2,1,0:T(1,128)S(1)}, u32[]{:S(2)}, u32[]{:S(2)}) collective-permute-start(f32[2,1,1024]{2,1,0:T(1,128)S(1)} %get-tuple-element.50), channel_id=1, source_target_pairs={{2,0},{4,2},{6,4},{8,6},{10,8},{12,10},{14,12},{16,14},{18,16},{20... | collective-permute-start | bytes 24584 | tf_op jit(solution)/shard_map/ppermute | solution.py:19
  134.2 0.0 collective-permute-done.10
  134.3 3.5 %collective-permute-done.11 = f32[2,1,1024]{2,1,0:T(1,128)S(1)} collective-permute-done((f32[2,1,1024]{2,1,0:T(1,128)S(1)}, f32[2,1,1024]{2,1,0:T(1,128)S(1)}, u32[]{:S(2)}, u32[]{:S(2)}) %collective-permute-start.11) | collective-permute-done | bytes 8224 | tf_op jit(solution)/shard_map/ppermute | solution.py:19
  137.7 0.1 select_maximum_fusion.10
  137.9 0.8 fusion.102
  138.7 0.8 broadcast_add_fusion
  (13 shorter events, 0.2 us)
Async XLA Ops:
  0.6 15.3 %copy-start = (f32[16,8,1024]{2,1,0:T(8,128)S(1)}, f32[16,8,1024]{2,1,0:T(8,128)}, u32[]{:S(2)}) copy-start(f32[16,8,1024]{2,1,0:T(8,128)} %param.5) | copy-start | bytes 1572868
  15.9 32.1 %copy-start.3 = (f32[5,12]{1,0:T(8,128)S(1)}, f32[5,12]{1,0:T(8,128)}, u32[]{:S(2)}) copy-start(f32[5,12]{1,0:T(8,128)} %param.9) | copy-start | bytes 724
  32.7 5.6 %collective-permute-start = (f32[2,16,1,1024]{3,2,1,0:T(1,128)S(1)}, f32[2,16,1,1024]{3,2,1,0:T(1,128)S(1)}, u32[]{:S(2)}, u32[]{:S(2)}) collective-permute-start(f32[2,16,1,1024]{3,2,1,0:T(1,128)S(1)} %get-tuple-element.41), channel_id=1, source_target_pairs={{0,2},{2,4},{4,6},{6,8},{8,10},{10,12},{12,14},{14,16},{16,18},{18... | collective-permute-start | bytes 393224 | tf_op jit(solution)/shard_map/ppermute | solution.py:16
  36.4 7.2 %collective-permute-start.1 = (f32[2,16,1,1024]{3,2,1,0:T(1,128)S(1)}, f32[2,16,1,1024]{3,2,1,0:T(1,128)S(1)}, u32[]{:S(2)}, u32[]{:S(2)}) collective-permute-start(f32[2,16,1,1024]{3,2,1,0:T(1,128)S(1)} %get-tuple-element.42), channel_id=1, source_target_pairs={{2,0},{4,2},{6,4},{8,6},{10,8},{12,10},{14,12},{16,14},{18,16},{20... | collective-permute-start | bytes 393224 | tf_op jit(solution)/shard_map/ppermute | solution.py:19
  43.6 5.2 %collective-permute-start.2 = (f32[2,1,10,1024]{3,2,1,0:T(8,128)S(1)}, f32[2,1,10,1024]{3,2,1,0:T(8,128)S(1)}, u32[]{:S(2)}, u32[]{:S(2)}) collective-permute-start(f32[2,1,10,1024]{3,2,1,0:T(8,128)S(1)} %get-tuple-element.37), channel_id=1, source_target_pairs={{0,1},{2,3},{4,5},{6,7},{8,9},{10,11},{12,13},{14,15},{16,17},{18,... | collective-permute-start | bytes 245768 | tf_op jit(solution)/shard_map/ppermute | solution.py:16
  46.7 5.7 %collective-permute-start.3 = (f32[2,1,10,1024]{3,2,1,0:T(8,128)S(1)}, f32[2,1,10,1024]{3,2,1,0:T(8,128)S(1)}, u32[]{:S(2)}, u32[]{:S(2)}) collective-permute-start(f32[2,1,10,1024]{3,2,1,0:T(8,128)S(1)} %get-tuple-element.38), channel_id=1, source_target_pairs={{1,0},{3,2},{5,4},{7,6},{9,8},{11,10},{13,12},{15,14},{17,16},{19,... | collective-permute-start | bytes 245768 | tf_op jit(solution)/shard_map/ppermute | solution.py:19
  54.0 1.0 copy-start.1
  54.0 1.2 copy-start.2
  75.8 6.2 %collective-permute-start.4 = (f32[2,16,1,1024]{3,2,1,0:T(1,128)S(1)}, f32[2,16,1,1024]{3,2,1,0:T(1,128)S(1)}, u32[]{:S(2)}, u32[]{:S(2)}) collective-permute-start(f32[2,16,1,1024]{3,2,1,0:T(1,128)S(1)} %get-tuple-element.39), channel_id=1, source_target_pairs={{0,2},{2,4},{4,6},{6,8},{8,10},{10,12},{12,14},{14,16},{16,18},{18... | collective-permute-start | bytes 393224 | tf_op jit(solution)/shard_map/ppermute | solution.py:16
  80.1 7.2 %collective-permute-start.5 = (f32[2,16,1,1024]{3,2,1,0:T(1,128)S(1)}, f32[2,16,1,1024]{3,2,1,0:T(1,128)S(1)}, u32[]{:S(2)}, u32[]{:S(2)}) collective-permute-start(f32[2,16,1,1024]{3,2,1,0:T(1,128)S(1)} %get-tuple-element.40), channel_id=1, source_target_pairs={{2,0},{4,2},{6,4},{8,6},{10,8},{12,10},{14,12},{16,14},{18,16},{20... | collective-permute-start | bytes 393224 | tf_op jit(solution)/shard_map/ppermute | solution.py:19
  87.3 3.2 %collective-permute-start.6 = (f32[2,1,10,1024]{3,2,1,0:T(8,128)S(1)}, f32[2,1,10,1024]{3,2,1,0:T(8,128)S(1)}, u32[]{:S(2)}, u32[]{:S(2)}) collective-permute-start(f32[2,1,10,1024]{3,2,1,0:T(8,128)S(1)} %get-tuple-element.35), channel_id=1, source_target_pairs={{0,1},{2,3},{4,5},{6,7},{8,9},{10,11},{12,13},{14,15},{16,17},{18,... | collective-permute-start | bytes 245768 | tf_op jit(solution)/shard_map/ppermute | solution.py:16
  88.6 5.7 %collective-permute-start.7 = (f32[2,1,10,1024]{3,2,1,0:T(8,128)S(1)}, f32[2,1,10,1024]{3,2,1,0:T(8,128)S(1)}, u32[]{:S(2)}, u32[]{:S(2)}) collective-permute-start(f32[2,1,10,1024]{3,2,1,0:T(8,128)S(1)} %get-tuple-element.36), channel_id=1, source_target_pairs={{1,0},{3,2},{5,4},{7,6},{9,8},{11,10},{13,12},{15,14},{17,16},{19,... | collective-permute-start | bytes 245768 | tf_op jit(solution)/shard_map/ppermute | solution.py:19
  119.4 6.2 %collective-permute-start.8 = (f32[2,1,1024]{2,1,0:T(1,128)S(1)}, f32[2,1,1024]{2,1,0:T(1,128)S(1)}, u32[]{:S(2)}, u32[]{:S(2)}) collective-permute-start(f32[2,1,1024]{2,1,0:T(1,128)S(1)} %get-tuple-element.51), channel_id=1, source_target_pairs={{0,2},{2,4},{4,6},{6,8},{8,10},{10,12},{12,14},{14,16},{16,18},{18... | collective-permute-start | bytes 24584 | tf_op jit(solution)/shard_map/ppermute | solution.py:16
  123.7 5.9 %collective-permute-start.9 = (f32[2,1,1024]{2,1,0:T(1,128)S(1)}, f32[2,1,1024]{2,1,0:T(1,128)S(1)}, u32[]{:S(2)}, u32[]{:S(2)}) collective-permute-start(f32[2,1,1024]{2,1,0:T(1,128)S(1)} %get-tuple-element.52), channel_id=1, source_target_pairs={{2,0},{4,2},{6,4},{8,6},{10,8},{12,10},{14,12},{16,14},{18,16},{20... | collective-permute-start | bytes 24584 | tf_op jit(solution)/shard_map/ppermute | solution.py:19
  129.9 4.3 %collective-permute-start.10 = (f32[2,1,1024]{2,1,0:T(1,128)S(1)}, f32[2,1,1024]{2,1,0:T(1,128)S(1)}, u32[]{:S(2)}, u32[]{:S(2)}) collective-permute-start(f32[2,1,1024]{2,1,0:T(1,128)S(1)} %get-tuple-element.49), channel_id=1, source_target_pairs={{0,2},{2,4},{4,6},{6,8},{8,10},{10,12},{12,14},{14,16},{16,18},{18... | collective-permute-start | bytes 24584 | tf_op jit(solution)/shard_map/ppermute | solution.py:16
  131.9 5.9 %collective-permute-start.11 = (f32[2,1,1024]{2,1,0:T(1,128)S(1)}, f32[2,1,1024]{2,1,0:T(1,128)S(1)}, u32[]{:S(2)}, u32[]{:S(2)}) collective-permute-start(f32[2,1,1024]{2,1,0:T(1,128)S(1)} %get-tuple-element.50), channel_id=1, source_target_pairs={{2,0},{4,2},{6,4},{8,6},{10,8},{12,10},{14,12},{16,14},{18,16},{20... | collective-permute-start | bytes 24584 | tf_op jit(solution)/shard_map/ppermute | solution.py:19
